TPU v7x, 32 devices: a whole 2x2x4 slice. The times are simulated.
32 devices in a mesh: gx: 8 (over y, x, core), gy: 4 (over z).
Axes of the slice: x: 2, y: 2, z: 4, core: 2. Of those that a mesh axis runs over, the one named last changes fastest.
Arguments:
- particle_count: int32 [8, 256, 1024], P(None, ('gx', 'gy')), may hold values from 0 to 12
- drag_coeff: float32 [8, 256, 1024], P(None, ('gx', 'gy')), may hold values from 0.05 to 2
- particle_velocity: float32 [3, 8, 256, 1024], P(None, None, ('gx', 'gy')), may hold values from -6 to 6
- fluid_velocity: float32 [3, 8, 256, 1024], P(None, None, 'gy', 'gx'), may hold values from -6 to 6
Outputs:
- pressure: float32 [8, 256, 1024], P(None, 'gy', 'gx')
- new_velocity: float32 [3, 8, 256, 1024], P(None, None, ('gx', 'gy'))
- pressure_gradient: float32 [3, 8, 256, 1024], P(None, None, ('gx', 'gy'))
All inputs are finite; a program needn't handle non-finite values.
Results may differ from a plain program's by a relative error of at most 0.00002.
Values sent between devices are 32-bit elements; how exact they have to be, the bound alone decides.
A program may use at most 64 MiB of HBM per device.

v0:
```python
import jax
import jax.numpy as jnp
from jax import lax
from jax.sharding import PartitionSpec as P

SWEEPS = 8


particle_volume = 0.05
time_step = 0.5
viscosity = 0.1


def padded_2(cells, sides, width):
    for axis, dim in sides:
        count = lax.axis_size(axis)
        ends = count - 1
        head = lax.slice_in_dim(cells, 0, width, axis=dim)
        tail = lax.slice_in_dim(cells, cells.shape[dim] - width, cells.shape[dim], axis=dim)
        cells = jnp.concatenate(
            [
                lax.ppermute(tail, axis, [(i, (i + 1) % count) for i in range(ends)]),
                cells,
                lax.ppermute(head, axis, [((i + 1) % count, i) for i in range(ends)]),
            ],
            axis=dim,
        )
    return cells


def pad_depth(values):
    widths = [(0, 0)] * (values.ndim - 3) + [(1, 1), (0, 0), (0, 0)]
    return jnp.pad(values, widths)


def pad_plane(values):
    widths = [(0, 0)] * (values.ndim - 2) + [(1, 1), (1, 1)]
    return jnp.pad(values, widths)


def pad_second(values):
    widths = [(0, 0)] * (values.ndim - 1) + [(1, 1)]
    return jnp.pad(values, widths)


def middle(values):
    return values[..., 1:-1, 1:-1, 1:-1]


def neighbour(values, which):
    if which == 0:
        return values[..., 2:, 1:-1, 1:-1]
    if which == 1:
        return values[..., :-2, 1:-1, 1:-1]
    if which == 2:
        return values[..., 1:-1, 2:, 1:-1]
    if which == 3:
        return values[..., 1:-1, :-2, 1:-1]
    if which == 4:
        return values[..., 1:-1, 1:-1, 2:]
    return values[..., 1:-1, 1:-1, :-2]


def face_weights(voids_wide):
    padded = pad_depth(voids_wide)
    centre = middle(padded)
    weights = jnp.stack([0.5 * (centre + neighbour(padded, which)) for which in range(6)])
    weight_sum = weights[0]
    for which in range(1, 6):
        weight_sum = weight_sum + weights[which]
    return (weights, weight_sum)


def momentum(velocity_wide, weights, voids, drag, drag_force):
    padded = pad_depth(velocity_wide)
    centre = middle(padded)
    diffusion = jnp.zeros_like(centre)
    for which in range(6):
        diffusion = diffusion + weights[which][None] * (neighbour(padded, which) - centre)
    return (voids[None] * centre + time_step * viscosity * diffusion + time_step * drag_force) / (
        voids[None] + time_step * drag[None]
    )


def divergence(flux_wide):
    first = flux_wide[0][:, 2:, 1:-1] - flux_wide[0][:, :-2, 1:-1]
    second = flux_wide[1][:, 1:-1, 2:] - flux_wide[1][:, 1:-1, :-2]
    normal = pad_depth(flux_wide[2])[:, 1:-1, 1:-1]
    third = normal[2:] - normal[:-2]
    return 0.5 * (first + second + third) / time_step


def jacobi_sweep(pressure_wide, weights, weight_sum, source):
    padded = pad_depth(pressure_wide)
    total = weights[0] * neighbour(padded, 0)
    for which in range(1, 6):
        total = total + weights[which] * neighbour(padded, which)
    return (total - source) / weight_sum


def gradient_of(pressure_wide):
    padded = pad_depth(pressure_wide)
    first = 0.5 * (padded[1:-1, 2:, 1:-1] - padded[1:-1, :-2, 1:-1])
    second = 0.5 * (padded[1:-1, 1:-1, 2:] - padded[1:-1, 1:-1, :-2])
    third = 0.5 * (padded[2:, 1:-1, 1:-1] - padded[:-2, 1:-1, 1:-1])
    return jnp.stack([first, second, third])


def order_inward(values, across, along):
    fields, planes, x_rows, y_cols = values.shape
    groups = across // along
    rows_each = x_rows // across
    shaped = values.reshape(fields, planes, along, groups, rows_each, y_cols)
    return jnp.swapaxes(shaped, 2, 3).reshape(fields, planes, x_rows, y_cols)


def order_outward(values, across, along):
    fields, planes, x_rows, y_cols = values.shape
    groups = across // along
    rows_each = x_rows // across
    shaped = values.reshape(fields, planes, groups, along, rows_each, y_cols)
    return jnp.swapaxes(shaped, 2, 3).reshape(fields, planes, x_rows, y_cols)


def to_fluid(fields):
    moved = lax.all_to_all(
        lax.all_to_all(fields, "gx", split_axis=3, concat_axis=2, tiled=True),
        "gy",
        split_axis=2,
        concat_axis=2,
        tiled=True,
    )
    return order_inward(moved, lax.axis_size("gx"), lax.axis_size("gy"))


def to_particles(fields):
    ordered = order_outward(fields, lax.axis_size("gx"), lax.axis_size("gy"))
    return lax.all_to_all(
        lax.all_to_all(ordered, "gy", split_axis=2, concat_axis=2, tiled=True),
        "gx",
        split_axis=2,
        concat_axis=3,
        tiled=True,
    )


def shards(particle_count, drag_coeff, particle_velocity, fluid_velocity):
    voids = 1.0 - particle_count.astype(jnp.float32) * particle_volume
    drag_force = drag_coeff[None] * particle_velocity
    slab_velocity = to_particles(fluid_velocity)
    stacked = jnp.concatenate([slab_velocity, voids[None]], axis=0)
    widened = pad_second(padded_2(stacked, ((("gx", "gy"), 2),), 1))
    weights, weight_sum = face_weights(widened[3])
    predicted = momentum(widened[:3], weights, voids, drag_coeff, drag_force)
    flux = voids[None] * predicted
    flux_first = pad_second(padded_2(flux[0:1], ((("gx", "gy"), 2),), 1))
    flux_wide = jnp.concatenate([flux_first, pad_plane(flux[1:3])], axis=0)
    source = divergence(flux_wide)
    pressure = -source / weight_sum
    for sweep_index in range(SWEEPS - 1):
        pressure_wide = pad_second(padded_2(pressure, ((("gx", "gy"), 1),), 1))
        pressure = jacobi_sweep(pressure_wide, weights, weight_sum, source)
    final_wide = pad_second(padded_2(pressure, ((("gx", "gy"), 1),), 1))
    slopes = gradient_of(final_wide)
    velocity = predicted - time_step * slopes
    pressure_out = to_fluid(pressure[None])[0]
    return (pressure_out, velocity, slopes)


def solution(mesh):
    placed = (
        P(None, ("gx", "gy"), None),
        P(None, ("gx", "gy"), None),
        P(None, None, ("gx", "gy"), None),
        P(None, None, "gy", "gx"),
    )
    return jax.shard_map(
        shards,
        mesh=mesh,
        in_specs=placed,
        out_specs=(
            P(None, "gy", "gx"),
            P(None, None, ("gx", "gy"), None),
            P(None, None, ("gx", "gy"), None),
        ),
        check_vma=False,
    )
```

profile of v0, /device:TPU:0, one launch (start us, length us, event | category | flops | bytes accessed | tf_op | source)
XLA Modules:
  0.0 200.9 jit_solution(16246067221753685963)
XLA Ops:
  0.6 1.2 copy.51
  1.8 0.5 copy.52
  2.3 26.5 %all_to_all.46 = f32[3,8,64,128]{3,1,0,2:T(8,128)} all-to-all(f32[3,8,64,128]{3,1,0,2:T(8,128)S(1)} %copy.52), channel_id=1, replica_groups=mesh['gx'=8,'gy'=4] {'gy'}, dimensions={2} | all-to-all | bytes 1572864 | tf_op jit(solution)/shard_map/all_to_all | solution.py:139
  28.8 3.7 %all-to-all-start.1 = ((f32[3,8,64,128]{3,1,0,2:T(8,128)}), f32[3,8,64,128]{3,1,0,2:T(8,128)S(1)}, u32[]{:S(2)}, u32[]{:S(2)}) async-start(f32[3,8,64,128]{3,1,0,2:T(8,128)} %all_to_all.46), calls=%async_computation.1 | async-start | bytes 1572864 | tf_op jit(solution)/shard_map/all_to_all | solution.py:138
  32.5 0.3 fusion.137
  32.9 12.2 %all-to-all-done.1 = f32[3,8,64,128]{3,1,0,2:T(8,128)S(1)} async-done(((f32[3,8,64,128]{3,1,0,2:T(8,128)}), f32[3,8,64,128]{3,1,0,2:T(8,128)S(1)}, u32[]{:S(2)}, u32[]{:S(2)}) %all-to-all-start.1) | async-done | bytes 786464 | tf_op jit(solution)/shard_map/all_to_all | solution.py:138
  45.2 2.1 %collective-permute-start = (f32[4,8,1,1024]{3,1,2,0:T(8,128)S(1)}, f32[4,8,1,1024]{3,1,2,0:T(8,128)S(1)}, u32[]{:S(2)}, u32[]{:S(2)}) collective-permute-start(f32[4,8,1,1024]{3,1,2,0:T(8,128)S(1)} %get-tuple-element.16), channel_id=1, source_target_pairs={{0,1},{1,2},{2,3},{3,4},{4,5},{5,6},{6,7},{7,8},{8,9},{9,10},{10,1... | collective-permute-start | bytes 393224 | tf_op jit(solution)/shard_map/ppermute | solution.py:22
  47.3 1.3 collective-permute-start.1
  48.6 1.2 collective-permute-done
  49.8 4.8 %collective-permute-done.1 = f32[4,8,1,1024]{3,1,2,0:T(8,128)S(1)} collective-permute-done((f32[4,8,1,1024]{3,1,2,0:T(8,128)S(1)}, f32[4,8,1,1024]{3,1,2,0:T(8,128)S(1)}, u32[]{:S(2)}, u32[]{:S(2)}) %collective-permute-start.1) | collective-permute-done | bytes 131104 | tf_op jit(solution)/shard_map/ppermute | solution.py:24
  54.7 0.4 select_maximum_fusion
  55.2 0.5 fusion.29
  55.7 0.6 copy-done
  56.4 1.4 broadcast_multiply_fusion
  57.8 2.5 %collective-permute-start.2 = (f32[1,8,1,1024]{3,1,2,0:T(8,128)S(1)}, f32[1,8,1,1024]{3,1,2,0:T(8,128)S(1)}, u32[]{:S(2)}, u32[]{:S(2)}) collective-permute-start(f32[1,8,1,1024]{3,1,2,0:T(8,128)S(1)} %get-tuple-element.20), channel_id=1, source_target_pairs={{0,1},{1,2},{2,3},{3,4},{4,5},{5,6},{6,7},{7,8},{8,9},{9,10},{10,1... | collective-permute-start | bytes 98312 | tf_op jit(solution)/shard_map/ppermute | solution.py:22
  60.3 1.3 collective-permute-start.3
  61.9 4.7 %collective-permute-done.3 = f32[1,8,1,1024]{3,1,2,0:T(8,128)S(1)} collective-permute-done((f32[1,8,1,1024]{3,1,2,0:T(8,128)S(1)}, f32[1,8,1,1024]{3,1,2,0:T(8,128)S(1)}, u32[]{:S(2)}, u32[]{:S(2)}) %collective-permute-start.3) | collective-permute-done | bytes 32800 | tf_op jit(solution)/shard_map/ppermute | solution.py:24
  66.8 0.4 fusion.124
  67.2 3.9 %collective-permute-start.4 = (f32[8,1,1024]{2,0,1:T(8,128)S(1)}, f32[8,1,1024]{2,0,1:T(8,128)S(1)}, u32[]{:S(2)}, u32[]{:S(2)}) collective-permute-start(f32[8,1,1024]{2,0,1:T(8,128)S(1)} %get-tuple-element.46), channel_id=1, source_target_pairs={{0,1},{1,2},{2,3},{3,4},{4,5},{5,6},{6,7},{7,8},{8,9},{9,10},{10,1... | collective-permute-start | bytes 98312 | tf_op jit(solution)/shard_map/ppermute | solution.py:22
  71.2 1.3 collective-permute-start.5
  72.5 0.3 collective-permute-done.4
  72.7 4.2 %collective-permute-done.5 = f32[8,1,1024]{2,0,1:T(8,128)S(1)} collective-permute-done((f32[8,1,1024]{2,0,1:T(8,128)S(1)}, f32[8,1,1024]{2,0,1:T(8,128)S(1)}, u32[]{:S(2)}, u32[]{:S(2)}) %collective-permute-start.5) | collective-permute-done | bytes 32800 | tf_op jit(solution)/shard_map/ppermute | solution.py:24
  77.1 0.4 fusion.39
  77.6 2.2 %collective-permute-start.6 = (f32[8,1,1024]{2,0,1:T(8,128)S(1)}, f32[8,1,1024]{2,0,1:T(8,128)S(1)}, u32[]{:S(2)}, u32[]{:S(2)}) collective-permute-start(f32[8,1,1024]{2,0,1:T(8,128)S(1)} %get-tuple-element.44), channel_id=1, source_target_pairs={{0,1},{1,2},{2,3},{3,4},{4,5},{5,6},{6,7},{7,8},{8,9},{9,10},{10,1... | collective-permute-start | bytes 98312 | tf_op jit(solution)/shard_map/ppermute | solution.py:22
  79.8 1.3 collective-permute-start.7
  81.1 0.3 collective-permute-done.6
  81.4 4.2 %collective-permute-done.7 = f32[8,1,1024]{2,0,1:T(8,128)S(1)} collective-permute-done((f32[8,1,1024]{2,0,1:T(8,128)S(1)}, f32[8,1,1024]{2,0,1:T(8,128)S(1)}, u32[]{:S(2)}, u32[]{:S(2)}) %collective-permute-start.7) | collective-permute-done | bytes 32800 | tf_op jit(solution)/shard_map/ppermute | solution.py:24
  85.8 0.4 fusion.48
  86.3 2.9 %collective-permute-start.8 = (f32[8,1,1024]{2,0,1:T(8,128)S(1)}, f32[8,1,1024]{2,0,1:T(8,128)S(1)}, u32[]{:S(2)}, u32[]{:S(2)}) collective-permute-start(f32[8,1,1024]{2,0,1:T(8,128)S(1)} %get-tuple-element.42), channel_id=1, source_target_pairs={{0,1},{1,2},{2,3},{3,4},{4,5},{5,6},{6,7},{7,8},{8,9},{9,10},{10,1... | collective-permute-start | bytes 98312 | tf_op jit(solution)/shard_map/ppermute | solution.py:22
  89.2 1.3 collective-permute-start.9
  90.8 4.2 %collective-permute-done.9 = f32[8,1,1024]{2,0,1:T(8,128)S(1)} collective-permute-done((f32[8,1,1024]{2,0,1:T(8,128)S(1)}, f32[8,1,1024]{2,0,1:T(8,128)S(1)}, u32[]{:S(2)}, u32[]{:S(2)}) %collective-permute-start.9) | collective-permute-done | bytes 32800 | tf_op jit(solution)/shard_map/ppermute | solution.py:24
  95.2 0.4 fusion.57
  95.6 4.1 %collective-permute-start.10 = (f32[8,1,1024]{2,0,1:T(8,128)S(1)}, f32[8,1,1024]{2,0,1:T(8,128)S(1)}, u32[]{:S(2)}, u32[]{:S(2)}) collective-permute-start(f32[8,1,1024]{2,0,1:T(8,128)S(1)} %get-tuple-element.40), channel_id=1, source_target_pairs={{0,1},{1,2},{2,3},{3,4},{4,5},{5,6},{6,7},{7,8},{8,9},{9,10},{10,1... | collective-permute-start | bytes 98312 | tf_op jit(solution)/shard_map/ppermute | solution.py:22
  99.7 1.3 collective-permute-start.11
  101.3 4.6 %collective-permute-done.11 = f32[8,1,1024]{2,0,1:T(8,128)S(1)} collective-permute-done((f32[8,1,1024]{2,0,1:T(8,128)S(1)}, f32[8,1,1024]{2,0,1:T(8,128)S(1)}, u32[]{:S(2)}, u32[]{:S(2)}) %collective-permute-start.11) | collective-permute-done | bytes 32800 | tf_op jit(solution)/shard_map/ppermute | solution.py:24
  106.1 0.4 fusion.66
  106.5 3.9 %collective-permute-start.12 = (f32[8,1,1024]{2,0,1:T(8,128)S(1)}, f32[8,1,1024]{2,0,1:T(8,128)S(1)}, u32[]{:S(2)}, u32[]{:S(2)}) collective-permute-start(f32[8,1,1024]{2,0,1:T(8,128)S(1)} %get-tuple-element.38), channel_id=1, source_target_pairs={{0,1},{1,2},{2,3},{3,4},{4,5},{5,6},{6,7},{7,8},{8,9},{9,10},{10,1... | collective-permute-start | bytes 98312 | tf_op jit(solution)/shard_map/ppermute | solution.py:22
  110.5 1.3 collective-permute-start.13
  112.1 4.6 %collective-permute-done.13 = f32[8,1,1024]{2,0,1:T(8,128)S(1)} collective-permute-done((f32[8,1,1024]{2,0,1:T(8,128)S(1)}, f32[8,1,1024]{2,0,1:T(8,128)S(1)}, u32[]{:S(2)}, u32[]{:S(2)}) %collective-permute-start.13) | collective-permute-done | bytes 32800 | tf_op jit(solution)/shard_map/ppermute | solution.py:24
  116.8 0.4 fusion.75
  117.3 3.7 %collective-permute-start.14 = (f32[8,1,1024]{2,0,1:T(8,128)S(1)}, f32[8,1,1024]{2,0,1:T(8,128)S(1)}, u32[]{:S(2)}, u32[]{:S(2)}) collective-permute-start(f32[8,1,1024]{2,0,1:T(8,128)S(1)} %get-tuple-element.36), channel_id=1, source_target_pairs={{0,1},{1,2},{2,3},{3,4},{4,5},{5,6},{6,7},{7,8},{8,9},{9,10},{10,1... | collective-permute-start | bytes 98312 | tf_op jit(solution)/shard_map/ppermute | solution.py:22
  121.0 1.3 collective-permute-start.15
  122.3 0.3 collective-permute-done.14
  122.6 4.6 %collective-permute-done.15 = f32[8,1,1024]{2,0,1:T(8,128)S(1)} collective-permute-done((f32[8,1,1024]{2,0,1:T(8,128)S(1)}, f32[8,1,1024]{2,0,1:T(8,128)S(1)}, u32[]{:S(2)}, u32[]{:S(2)}) %collective-permute-start.15) | collective-permute-done | bytes 32800 | tf_op jit(solution)/shard_map/ppermute | solution.py:24
  127.3 0.4 fusion.84
  127.7 3.7 %collective-permute-start.16 = (f32[8,1,1024]{2,0,1:T(8,128)S(1)}, f32[8,1,1024]{2,0,1:T(8,128)S(1)}, u32[]{:S(2)}, u32[]{:S(2)}) collective-permute-start(f32[8,1,1024]{2,0,1:T(8,128)S(1)} %get-tuple-element.34), channel_id=1, source_target_pairs={{0,1},{1,2},{2,3},{3,4},{4,5},{5,6},{6,7},{7,8},{8,9},{9,10},{10,1... | collective-permute-start | bytes 98312 | tf_op jit(solution)/shard_map/ppermute | solution.py:22
  131.5 1.3 collective-permute-start.17
  133.0 4.6 %collective-permute-done.17 = f32[8,1,1024]{2,0,1:T(8,128)S(1)} collective-permute-done((f32[8,1,1024]{2,0,1:T(8,128)S(1)}, f32[8,1,1024]{2,0,1:T(8,128)S(1)}, u32[]{:S(2)}, u32[]{:S(2)}) %collective-permute-start.17) | collective-permute-done | bytes 32800 | tf_op jit(solution)/shard_map/ppermute | solution.py:24
  137.8 0.4 fusion.93
  138.2 1.3 collective-permute-start.18
  139.5 4.5 %collective-permute-start.19 = (f32[8,1,1024]{2,0,1:T(8,128)S(1)}, f32[8,1,1024]{2,0,1:T(8,128)S(1)}, u32[]{:S(2)}, u32[]{:S(2)}) collective-permute-start(f32[8,1,1024]{2,0,1:T(8,128)S(1)} %get-tuple-element.32), channel_id=1, source_target_pairs={{0,1},{1,2},{2,3},{3,4},{4,5},{5,6},{6,7},{7,8},{8,9},{9,10},{10,1... | collective-permute-start | bytes 98312 | tf_op jit(solution)/shard_map/ppermute | solution.py:22
  144.1 2.7 %copy.58 = f32[1,8,8,1024]{2,1,0,3:T(8,128)} copy(f32[1,8,8,1024]{3,1,2,0:T(8,128)S(1)} %bitcast.42) | data formatting | bytes 524288 | tf_op jit(solution)/shard_map/broadcast_in_dim | solution.py:166
  146.8 4.4 %reshape.29 = f32[8,1,8192]{2,1,0:T(1,128)} reshape(f32[1024,1,8,8]{3,2,1,0:T(8,128)} %bitcast.38) | data formatting | bytes 524288
  151.2 18.5 %all-to-all-start.2 = ((f32[8,1,8192]{2,1,0:T(1,128)}), f32[8,1,8192]{2,1,0:T(1,128)S(1)}, u32[]{:S(2)}, u32[]{:S(2)}) async-start(f32[8,1,8192]{2,1,0:T(1,128)} %reshape.29), calls=%async_computation.2 | async-start | bytes 524288 | tf_op jit(solution)/shard_map/all_to_all | solution.py:127
  169.8 6.7 %all-to-all-done.2 = f32[8,1,8192]{2,1,0:T(1,128)S(1)} async-done(((f32[8,1,8192]{2,1,0:T(1,128)}), f32[8,1,8192]{2,1,0:T(1,128)S(1)}, u32[]{:S(2)}, u32[]{:S(2)}) %all-to-all-start.2) | async-done | bytes 262176 | tf_op jit(solution)/shard_map/all_to_all | solution.py:127
  176.5 0.5 broadcast.218
  177.1 1.3 reduce
  178.4 4.3 %reshape.30 = f32[1024,1,8,8]{3,2,1,0:T(8,128)} reshape(f32[8,8192]{1,0:T(8,128)S(1)} %reduce) | data formatting | bytes 524288
  182.7 3.5 %copy.59 = f32[1,8,8,8,128]{4,1,3,2,0:T(8,128)} copy(f32[1,8,8,8,128]{3,1,4,2,0:T(8,128)} %bitcast.37) | data formatting | bytes 524288 | tf_op jit(solution)/shard_map/all_to_all | solution.py:127
  186.1 5.7 %all-to-all-start.3 = ((f32[1,8,64,128]{3,1,0,2:T(8,128)}), f32[1,8,64,128]{3,1,0,2:T(8,128)S(1)}, u32[]{:S(2)}, u32[]{:S(2)}) async-start(f32[1,8,64,128]{3,1,0,2:T(8,128)} %bitcast.14), calls=%async_computation.3 | async-start | bytes 524288 | tf_op jit(solution)/shard_map/all_to_all | solution.py:126
  192.2 1.3 copy.62
  193.6 1.3 copy.63
  194.9 5.2 %all-to-all-done.3 = f32[1,8,64,128]{3,1,0,2:T(8,128)S(1)} async-done(((f32[1,8,64,128]{3,1,0,2:T(8,128)}), f32[1,8,64,128]{3,1,0,2:T(8,128)S(1)}, u32[]{:S(2)}, u32[]{:S(2)}) %all-to-all-start.3) | async-done | bytes 262176 | tf_op jit(solution)/shard_map/all_to_all | solution.py:126
  200.2 0.7 copy.61
  (40 shorter events, 3.6 us)
Async XLA Ops:
  2.3 30.2 %copy-start.1 = (f32[8,8,1024]{2,1,0:T(8,128)S(1)}, f32[8,8,1024]{2,1,0:T(8,128)}, u32[]{:S(2)}) copy-start(f32[8,8,1024]{2,1,0:T(8,128)} %param.5) | copy-start | bytes 786436
  2.3 30.2 %copy-start.2 = (s32[8,8,1024]{2,1,0:T(8,128)S(1)}, s32[8,8,1024]{2,1,0:T(8,128)}, u32[]{:S(2)}) copy-start(s32[8,8,1024]{2,1,0:T(8,128)} %param.4) | copy-start | bytes 786436
  28.8 16.3 %all-to-all-start.1 = ((f32[3,8,64,128]{3,1,0,2:T(8,128)}), f32[3,8,64,128]{3,1,0,2:T(8,128)S(1)}, u32[]{:S(2)}, u32[]{:S(2)}) async-start(f32[3,8,64,128]{3,1,0,2:T(8,128)} %all_to_all.46), calls=%async_computation.1 | async-start | bytes 1572864 | tf_op jit(solution)/shard_map/all_to_all | solution.py:138
  45.2 4.6 %collective-permute-start = (f32[4,8,1,1024]{3,1,2,0:T(8,128)S(1)}, f32[4,8,1,1024]{3,1,2,0:T(8,128)S(1)}, u32[]{:S(2)}, u32[]{:S(2)}) collective-permute-start(f32[4,8,1,1024]{3,1,2,0:T(8,128)S(1)} %get-tuple-element.16), channel_id=1, source_target_pairs={{0,1},{1,2},{2,3},{3,4},{4,5},{5,6},{6,7},{7,8},{8,9},{9,10},{10,1... | collective-permute-start | bytes 393224 | tf_op jit(solution)/shard_map/ppermute | solution.py:22
  47.3 7.3 %collective-permute-start.1 = (f32[4,8,1,1024]{3,1,2,0:T(8,128)S(1)}, f32[4,8,1,1024]{3,1,2,0:T(8,128)S(1)}, u32[]{:S(2)}, u32[]{:S(2)}) collective-permute-start(f32[4,8,1,1024]{3,1,2,0:T(8,128)S(1)} %get-tuple-element.17), channel_id=1, source_target_pairs={{1,0},{2,1},{3,2},{4,3},{5,4},{6,5},{7,6},{8,7},{9,8},{10,9},{11,1... | collective-permute-start | bytes 393224 | tf_op jit(solution)/shard_map/ppermute | solution.py:24
  55.2 1.1 copy-start
  57.8 4.1 %collective-permute-start.2 = (f32[1,8,1,1024]{3,1,2,0:T(8,128)S(1)}, f32[1,8,1,1024]{3,1,2,0:T(8,128)S(1)}, u32[]{:S(2)}, u32[]{:S(2)}) collective-permute-start(f32[1,8,1,1024]{3,1,2,0:T(8,128)S(1)} %get-tuple-element.20), channel_id=1, source_target_pairs={{0,1},{1,2},{2,3},{3,4},{4,5},{5,6},{6,7},{7,8},{8,9},{9,10},{10,1... | collective-permute-start | bytes 98312 | tf_op jit(solution)/shard_map/ppermute | solution.py:22
  60.3 6.3 %collective-permute-start.3 = (f32[1,8,1,1024]{3,1,2,0:T(8,128)S(1)}, f32[1,8,1,1024]{3,1,2,0:T(8,128)S(1)}, u32[]{:S(2)}, u32[]{:S(2)}) collective-permute-start(f32[1,8,1,1024]{3,1,2,0:T(8,128)S(1)} %get-tuple-element.21), channel_id=1, source_target_pairs={{1,0},{2,1},{3,2},{4,3},{5,4},{6,5},{7,6},{8,7},{9,8},{10,9},{11,1... | collective-permute-start | bytes 98312 | tf_op jit(solution)/shard_map/ppermute | solution.py:24
  67.2 5.5 %collective-permute-start.4 = (f32[8,1,1024]{2,0,1:T(8,128)S(1)}, f32[8,1,1024]{2,0,1:T(8,128)S(1)}, u32[]{:S(2)}, u32[]{:S(2)}) collective-permute-start(f32[8,1,1024]{2,0,1:T(8,128)S(1)} %get-tuple-element.46), channel_id=1, source_target_pairs={{0,1},{1,2},{2,3},{3,4},{4,5},{5,6},{6,7},{7,8},{8,9},{9,10},{10,1... | collective-permute-start | bytes 98312 | tf_op jit(solution)/shard_map/ppermute | solution.py:22
  71.2 5.8 %collective-permute-start.5 = (f32[8,1,1024]{2,0,1:T(8,128)S(1)}, f32[8,1,1024]{2,0,1:T(8,128)S(1)}, u32[]{:S(2)}, u32[]{:S(2)}) collective-permute-start(f32[8,1,1024]{2,0,1:T(8,128)S(1)} %get-tuple-element.47), channel_id=1, source_target_pairs={{1,0},{2,1},{3,2},{4,3},{5,4},{6,5},{7,6},{8,7},{9,8},{10,9},{11,1... | collective-permute-start | bytes 98312 | tf_op jit(solution)/shard_map/ppermute | solution.py:24
  77.6 3.8 %collective-permute-start.6 = (f32[8,1,1024]{2,0,1:T(8,128)S(1)}, f32[8,1,1024]{2,0,1:T(8,128)S(1)}, u32[]{:S(2)}, u32[]{:S(2)}) collective-permute-start(f32[8,1,1024]{2,0,1:T(8,128)S(1)} %get-tuple-element.44), channel_id=1, source_target_pairs={{0,1},{1,2},{2,3},{3,4},{4,5},{5,6},{6,7},{7,8},{8,9},{9,10},{10,1... | collective-permute-start | bytes 98312 | tf_op jit(solution)/shard_map/ppermute | solution.py:22
  79.8 5.8 %collective-permute-start.7 = (f32[8,1,1024]{2,0,1:T(8,128)S(1)}, f32[8,1,1024]{2,0,1:T(8,128)S(1)}, u32[]{:S(2)}, u32[]{:S(2)}) collective-permute-start(f32[8,1,1024]{2,0,1:T(8,128)S(1)} %get-tuple-element.45), channel_id=1, source_target_pairs={{1,0},{2,1},{3,2},{4,3},{5,4},{6,5},{7,6},{8,7},{9,8},{10,9},{11,1... | collective-permute-start | bytes 98312 | tf_op jit(solution)/shard_map/ppermute | solution.py:24
  86.3 4.5 %collective-permute-start.8 = (f32[8,1,1024]{2,0,1:T(8,128)S(1)}, f32[8,1,1024]{2,0,1:T(8,128)S(1)}, u32[]{:S(2)}, u32[]{:S(2)}) collective-permute-start(f32[8,1,1024]{2,0,1:T(8,128)S(1)} %get-tuple-element.42), channel_id=1, source_target_pairs={{0,1},{1,2},{2,3},{3,4},{4,5},{5,6},{6,7},{7,8},{8,9},{9,10},{10,1... | collective-permute-start | bytes 98312 | tf_op jit(solution)/shard_map/ppermute | solution.py:22
  89.2 5.8 %collective-permute-start.9 = (f32[8,1,1024]{2,0,1:T(8,128)S(1)}, f32[8,1,1024]{2,0,1:T(8,128)S(1)}, u32[]{:S(2)}, u32[]{:S(2)}) collective-permute-start(f32[8,1,1024]{2,0,1:T(8,128)S(1)} %get-tuple-element.43), channel_id=1, source_target_pairs={{1,0},{2,1},{3,2},{4,3},{5,4},{6,5},{7,6},{8,7},{9,8},{10,9},{11,1... | collective-permute-start | bytes 98312 | tf_op jit(solution)/shard_map/ppermute | solution.py:24
  95.6 5.7 %collective-permute-start.10 = (f32[8,1,1024]{2,0,1:T(8,128)S(1)}, f32[8,1,1024]{2,0,1:T(8,128)S(1)}, u32[]{:S(2)}, u32[]{:S(2)}) collective-permute-start(f32[8,1,1024]{2,0,1:T(8,128)S(1)} %get-tuple-element.40), channel_id=1, source_target_pairs={{0,1},{1,2},{2,3},{3,4},{4,5},{5,6},{6,7},{7,8},{8,9},{9,10},{10,1... | collective-permute-start | bytes 98312 | tf_op jit(solution)/shard_map/ppermute | solution.py:22
  99.7 6.2 %collective-permute-start.11 = (f32[8,1,1024]{2,0,1:T(8,128)S(1)}, f32[8,1,1024]{2,0,1:T(8,128)S(1)}, u32[]{:S(2)}, u32[]{:S(2)}) collective-permute-start(f32[8,1,1024]{2,0,1:T(8,128)S(1)} %get-tuple-element.41), channel_id=1, source_target_pairs={{1,0},{2,1},{3,2},{4,3},{5,4},{6,5},{7,6},{8,7},{9,8},{10,9},{11,1... | collective-permute-start | bytes 98312 | tf_op jit(solution)/shard_map/ppermute | solution.py:24
  106.5 5.5 %collective-permute-start.12 = (f32[8,1,1024]{2,0,1:T(8,128)S(1)}, f32[8,1,1024]{2,0,1:T(8,128)S(1)}, u32[]{:S(2)}, u32[]{:S(2)}) collective-permute-start(f32[8,1,1024]{2,0,1:T(8,128)S(1)} %get-tuple-element.38), channel_id=1, source_target_pairs={{0,1},{1,2},{2,3},{3,4},{4,5},{5,6},{6,7},{7,8},{8,9},{9,10},{10,1... | collective-permute-start | bytes 98312 | tf_op jit(solution)/shard_map/ppermute | solution.py:22
  110.5 6.1 %collective-permute-start.13 = (f32[8,1,1024]{2,0,1:T(8,128)S(1)}, f32[8,1,1024]{2,0,1:T(8,128)S(1)}, u32[]{:S(2)}, u32[]{:S(2)}) collective-permute-start(f32[8,1,1024]{2,0,1:T(8,128)S(1)} %get-tuple-element.39), channel_id=1, source_target_pairs={{1,0},{2,1},{3,2},{4,3},{5,4},{6,5},{7,6},{8,7},{9,8},{10,9},{11,1... | collective-permute-start | bytes 98312 | tf_op jit(solution)/shard_map/ppermute | solution.py:24
  117.3 5.3 %collective-permute-start.14 = (f32[8,1,1024]{2,0,1:T(8,128)S(1)}, f32[8,1,1024]{2,0,1:T(8,128)S(1)}, u32[]{:S(2)}, u32[]{:S(2)}) collective-permute-start(f32[8,1,1024]{2,0,1:T(8,128)S(1)} %get-tuple-element.36), channel_id=1, source_target_pairs={{0,1},{1,2},{2,3},{3,4},{4,5},{5,6},{6,7},{7,8},{8,9},{9,10},{10,1... | collective-permute-start | bytes 98312 | tf_op jit(solution)/shard_map/ppermute | solution.py:22
  121.0 6.1 %collective-permute-start.15 = (f32[8,1,1024]{2,0,1:T(8,128)S(1)}, f32[8,1,1024]{2,0,1:T(8,128)S(1)}, u32[]{:S(2)}, u32[]{:S(2)}) collective-permute-start(f32[8,1,1024]{2,0,1:T(8,128)S(1)} %get-tuple-element.37), channel_id=1, source_target_pairs={{1,0},{2,1},{3,2},{4,3},{5,4},{6,5},{7,6},{8,7},{9,8},{10,9},{11,1... | collective-permute-start | bytes 98312 | tf_op jit(solution)/shard_map/ppermute | solution.py:24
  127.7 5.3 %collective-permute-start.16 = (f32[8,1,1024]{2,0,1:T(8,128)S(1)}, f32[8,1,1024]{2,0,1:T(8,128)S(1)}, u32[]{:S(2)}, u32[]{:S(2)}) collective-permute-start(f32[8,1,1024]{2,0,1:T(8,128)S(1)} %get-tuple-element.34), channel_id=1, source_target_pairs={{0,1},{1,2},{2,3},{3,4},{4,5},{5,6},{6,7},{7,8},{8,9},{9,10},{10,1... | collective-permute-start | bytes 98312 | tf_op jit(solution)/shard_map/ppermute | solution.py:22
  131.5 6.1 %collective-permute-start.17 = (f32[8,1,1024]{2,0,1:T(8,128)S(1)}, f32[8,1,1024]{2,0,1:T(8,128)S(1)}, u32[]{:S(2)}, u32[]{:S(2)}) collective-permute-start(f32[8,1,1024]{2,0,1:T(8,128)S(1)} %get-tuple-element.35), channel_id=1, source_target_pairs={{1,0},{2,1},{3,2},{4,3},{5,4},{6,5},{7,6},{8,7},{9,8},{10,9},{11,1... | collective-permute-start | bytes 98312 | tf_op jit(solution)/shard_map/ppermute | solution.py:24
  138.2 31.4 %collective-permute-start.18 = (f32[8,1,1024]{2,0,1:T(8,128)S(1)}, f32[8,1,1024]{2,0,1:T(8,128)S(1)}, u32[]{:S(2)}, u32[]{:S(2)}) collective-permute-start(f32[8,1,1024]{2,0,1:T(8,128)S(1)} %get-tuple-element.33), channel_id=1, source_target_pairs={{1,0},{2,1},{3,2},{4,3},{5,4},{6,5},{7,6},{8,7},{9,8},{10,9},{11,1... | collective-permute-start | bytes 98312 | tf_op jit(solution)/shard_map/ppermute | solution.py:24
  139.5 30.1 %collective-permute-start.19 = (f32[8,1,1024]{2,0,1:T(8,128)S(1)}, f32[8,1,1024]{2,0,1:T(8,128)S(1)}, u32[]{:S(2)}, u32[]{:S(2)}) collective-permute-start(f32[8,1,1024]{2,0,1:T(8,128)S(1)} %get-tuple-element.32), channel_id=1, source_target_pairs={{0,1},{1,2},{2,3},{3,4},{4,5},{5,6},{6,7},{7,8},{8,9},{9,10},{10,1... | collective-permute-start | bytes 98312 | tf_op jit(solution)/shard_map/ppermute | solution.py:22
  151.2 25.4 %all-to-all-start.2 = ((f32[8,1,8192]{2,1,0:T(1,128)}), f32[8,1,8192]{2,1,0:T(1,128)S(1)}, u32[]{:S(2)}, u32[]{:S(2)}) async-start(f32[8,1,8192]{2,1,0:T(1,128)} %reshape.29), calls=%async_computation.2 | async-start | bytes 524288 | tf_op jit(solution)/shard_map/all_to_all | solution.py:127
  186.1 14.0 %all-to-all-start.3 = ((f32[1,8,64,128]{3,1,0,2:T(8,128)}), f32[1,8,64,128]{3,1,0,2:T(8,128)S(1)}, u32[]{:S(2)}, u32[]{:S(2)}) async-start(f32[1,8,64,128]{3,1,0,2:T(8,128)} %bitcast.14), calls=%async_computation.3 | async-start | bytes 524288 | tf_op jit(solution)/shard_map/all_to_all | solution.py:126
where the time goes:
time: 202 us; the launch traced here: 201 us
  starting transfers between devices  74.5 us (37%)
  waiting for transfers between devices  67.8 us (34%)
  blocking collectives  26.5 us (13%)
  local copies, waits for them, and re-layouts  21.6 us (11%)
  other arithmetic  9.39 us (5%)
    ppermute x10, waiting for transfers between devices, padded_2(): lax.ppermute(head, axis, [((i + 1) % count, i) for i in range(ends)])  40.5 us
    ppermute x10, starting transfers between devices, padded_2(): lax.ppermute(tail, axis, [(i, (i + 1) % count) for i in range(ends)])  33.7 us
    all_to_all x1, blocking collectives, to_particles(): lax.all_to_all(ordered, 'gy', split_axis=2, concat_axis=2, tiled=True)  26.5 us
    all_to_all x1, starting transfers between devices, to_fluid(): lax.all_to_all(fields, 'gx', split_axis=3, concat_axis=2, tiled=True)  18.5 us
    ppermute x10, starting transfers between devices, padded_2(): lax.ppermute(head, axis, [((i + 1) % count, i) for i in range(ends)])  12.9 us
    all_to_all x1, waiting for transfers between devices, to_particles(): lax.all_to_all(lax.all_to_all(ordered, 'gy', split_axis=2, concat_axis=2,...  12.2 us
    unnamed x10, local copies, waits for them, and re-layouts  12.1 us
    all_to_all x1, waiting for transfers between devices, to_fluid(): lax.all_to_all(fields, 'gx', split_axis=3, concat_axis=2, tiled=True)  6.72 us
  transfers between devices with their start and end apart: 23, of which 20 were waited for; matrix products, arithmetic and copies ran while one was open for 5% of the time, Pallas kernels for 0%

commit v1 on v0

v1 whole, which is shorter than its diff:
```python
import functools

import jax
import jax.numpy as jnp
from jax import lax
from jax.experimental import pallas as pl
from jax.experimental.pallas import tpu as pltpu
from jax.sharding import PartitionSpec as P

SWEEPS = 8
ROUNDS = (4, 4)

particle_volume = 0.05
time_step = 0.5
viscosity = 0.1


def kernel(
    K, G, R, NZ, NY, W,
    count_in, drag_in, pvel_in, fluid_in,
    press_out, vel_out, grad_out,
    fp, z0, z1, u0, u12, cn, dr, pv0, pv12, vo, rh, pred, fl, b, pm, t0, t1, pf, po,
    loc_sem, fh_send, fh_recv, s1_send, s1_recv, s2_send, s2_recv,
    hal_send, hal_recv, pr_send, pr_recv, out_send, out_recv,
):
    H = ROUNDS[0]
    C = G // K
    B = C * K
    x = lax.axis_index("gx")
    k = lax.axis_index("gy")
    place = x * K + k
    has_prev = place > 0
    has_next = place < G * K - 1
    prev_id = {"gx": jnp.where(k > 0, x, jnp.maximum(x - 1, 0)), "gy": lax.rem(k + K - 1, K)}
    next_id = {"gx": jnp.where(k < K - 1, x, jnp.minimum(x + 1, G - 1)), "gy": lax.rem(k + 1, K)}

    def remote(src, dst, ssem, rsem, to):
        return pltpu.make_async_remote_copy(
            src_ref=src, dst_ref=dst, send_sem=ssem, recv_sem=rsem, device_id=to, device_id_type=pl.DeviceIdType.MESH
        )

    rows = R * B

    up = {"gx": x, "gy": lax.rem(k + K - 1, K)}
    down = {"gx": x, "gy": lax.rem(k + 1, K)}
    to_up = remote(fluid_in.at[:, 0:2], fp.at[:, rows + 2:rows + 4], fh_send.at[0], fh_recv.at[0], up)
    to_down = remote(fluid_in.at[:, rows - 2:rows], fp.at[:, 0:2], fh_send.at[1], fh_recv.at[1], down)

    @pl.when(k > 0)
    def _():
        to_up.start()

    @pl.when(k < K - 1)
    def _():
        to_down.start()

    local = [
        pltpu.make_async_copy(fluid_in, fp.at[:, 2:rows + 2], loc_sem.at[0]),
        pltpu.make_async_copy(count_in, cn.at[H:H + R], loc_sem.at[1]),
        pltpu.make_async_copy(drag_in, dr.at[1:R + 1], loc_sem.at[2]),
        pltpu.make_async_copy(pvel_in.at[0], pv0.at[1:R + 1], loc_sem.at[3]),
        pltpu.make_async_copy(pvel_in.at[1:3], pv12, loc_sem.at[4]),
    ]
    for copy in local:
        copy.start()

    halo_up = [
        remote(count_in.at[0:H], cn.at[H + R:2 * H + R], hal_send.at[0], hal_recv.at[0], prev_id),
        remote(drag_in.at[0:1], dr.at[R + 1:R + 2], hal_send.at[1], hal_recv.at[1], prev_id),
        remote(pvel_in.at[0, 0:1], pv0.at[R + 1:R + 2], hal_send.at[2], hal_recv.at[2], prev_id),
    ]
    halo_down = [
        remote(count_in.at[R - H:R], cn.at[0:H], hal_send.at[3], hal_recv.at[3], next_id),
        remote(drag_in.at[R - 1:R], dr.at[0:1], hal_send.at[4], hal_recv.at[4], next_id),
        remote(pvel_in.at[0, R - 1:R], pv0.at[0:1], hal_send.at[5], hal_recv.at[5], next_id),
    ]

    @pl.when(k == 0)
    def _():
        fp[:, 0:2] = jnp.zeros((3, 2, NZ, W), jnp.float32)

    @pl.when(k == K - 1)
    def _():
        fp[:, rows + 2:rows + 4] = jnp.zeros((3, 2, NZ, W), jnp.float32)

    edge = jnp.zeros((H, NZ, NY), jnp.float32)

    @pl.when(jnp.logical_not(has_prev))
    def _():
        b[0:H] = edge
        pm[0:H] = edge

    @pl.when(jnp.logical_not(has_next))
    def _():
        b[H + R:2 * H + R] = edge
        pm[H + R:2 * H + R] = edge

    local[0].wait()

    @pl.when(k < K - 1)
    def _():
        to_up.wait_recv()

    @pl.when(k > 0)
    def _():
        to_down.wait_recv()

    def part0(at):
        return fp.at[0, pl.ds(at * R, R + 4)]

    def part1(at):
        return fp.at[1:3, pl.ds(at * R + 1, R + 2)]

    first = []
    for d in range(1, K):
        j = lax.rem(k + d, K)
        to = {"gx": x, "gy": j}
        pair = []
        for c in range(C):
            n = ((d - 1) * C + c) * 2
            pair.append(remote(part0(c * K + j), z0.at[d - 1, c], s1_send.at[n], s1_recv.at[n], to))
            pair.append(remote(part1(c * K + j), z1.at[d - 1, c], s1_send.at[n + 1], s1_recv.at[n + 1], to))
        for copy in pair:
            copy.start()
        first.append(pair)

    columns = pl.ds(pl.multiple_of(x * W, W), W)
    second = []
    for d in range(K):
        source = lax.rem(k + K - d, K)
        if d > 0:
            for copy in first[d - 1]:
                copy.wait_recv()
        for c in range(C):
            target = source * C + c
            n = (d * C + c) * 2
            src0 = part0(c * K + k) if d == 0 else z0.at[d - 1, c]
            src1 = part1(c * K + k) if d == 0 else z1.at[d - 1, c]
            dst0 = u0.at[:, :, columns]
            dst1 = u12.at[:, :, :, columns]
            to = {"gx": target, "gy": k}
            far0 = remote(src0, dst0, s2_send.at[n], s2_recv.at[2 * x], to)
            far1 = remote(src1, dst1, s2_send.at[n + 1], s2_recv.at[2 * x + 1], to)
            near0 = pltpu.make_async_copy(src0, dst0, s2_recv.at[2 * x])
            near1 = pltpu.make_async_copy(src1, dst1, s2_recv.at[2 * x + 1])

            @pl.when(target != x)
            def _(far0=far0, far1=far1):
                far0.start()
                far1.start()

            @pl.when(target == x)
            def _(near0=near0, near1=near1):
                near0.start()
                near1.start()

            second.append((target, far0, far1))
        if d == 0:
            @pl.when(has_prev)
            def _():
                for copy in halo_up:
                    copy.start()

            @pl.when(has_next)
            def _():
                for copy in halo_down:
                    copy.start()

    for copy in local[1:]:
        copy.wait()

    @pl.when(has_next)
    def _():
        for copy in halo_up:
            copy.wait_recv()

    @pl.when(has_prev)
    def _():
        for copy in halo_down:
            copy.wait_recv()

    lane = lax.broadcasted_iota(jnp.int32, (NZ, NY), 1)
    level = lax.broadcasted_iota(jnp.int32, (NZ, NY), 0)

    def above(v):
        return jnp.where(level < NZ - 1, pltpu.roll(v, NZ - 1, 0), 0.0)

    def below(v):
        return jnp.where(level > 0, pltpu.roll(v, 1, 0), 0.0)

    def right(v):
        return jnp.where(lane < NY - 1, pltpu.roll(v, NY - 1, 1), 0.0)

    def left(v):
        return jnp.where(lane > 0, pltpu.roll(v, 1, 1), 0.0)

    def plane_sum(v):
        return above(v) + below(v) + right(v) + left(v)

    def inside(i):
        at = place * R + i
        return jnp.logical_and(at >= 0, at < G * K * R)

    def voids_row(n, carry):
        v = 1.0 - cn[n].astype(jnp.float32) * particle_volume
        vo[n] = jnp.where(inside(n - H), v, 0.0)
        return carry

    lax.fori_loop(0, R + 2 * H, voids_row, 0)

    def weight_row(n, carry):
        v = vo[n]
        ws = 0.5 * (6.0 * v + vo[n - 1] + vo[n + 1] + plane_sum(v))
        rh[n] = jnp.where(inside(n - H), 1.0 / ws, 0.0)
        return carry

    lax.fori_loop(1, R + 2 * H - 1, weight_row, 0)

    for sender in range(G):
        spot = pl.ds(sender * W, W)
        here = {"gx": x, "gy": k}
        remote(z0.at[0, 0], u0.at[:, :, spot], s2_send.at[0], s2_recv.at[2 * sender], here).wait_recv()
        remote(z1.at[0, 0], u12.at[:, :, :, spot], s2_send.at[1], s2_recv.at[2 * sender + 1], here).wait_recv()

    def predict(i, u_of, force):
        v, va, vb = vo[H + i], vo[H + i - 1], vo[H + i + 1]
        ps = plane_sum(v)
        ws = 0.5 * (6.0 * v + va + vb + ps)
        u, ua, ub = u_of(i), u_of(i - 1), u_of(i + 1)
        near = ua + ub + plane_sum(u)
        nearv = va * ua + vb * ub + plane_sum(v * u)
        diffusion = 0.5 * (v * near + nearv) - ws * u
        drag = dr[i + 1]
        return (v * u + (time_step * viscosity) * diffusion + time_step * (drag * force)) / (v + time_step * drag)

    def first_row(n, carry):
        i = n - 1
        value = predict(i, lambda m: u0[m + 2], pv0[n])
        fl[n] = jnp.where(inside(i), vo[H + i] * value, 0.0)
        pred[0, n] = value
        return carry

    lax.fori_loop(0, R + 2, first_row, 0)

    def source_row(i, carry):
        v = vo[H + i]
        p1 = predict(i, lambda m: u12[0, m + 1], pv12[0, i])
        pred[1, i + 1] = p1
        f1 = v * p1
        p2 = predict(i, lambda m: u12[1, m + 1], pv12[1, i])
        pred[2, i + 1] = p2
        f2 = v * p2
        source = (fl[i + 2] - fl[i]) + (right(f1) - left(f1)) + (above(f2) - below(f2))
        b[H + i] = -source * rh[H + i]
        return carry

    lax.fori_loop(0, R, source_row, 0)

    def sweep(src, dst, reach):
        def row(n, carry):
            p, pa, pb = src[n], src[n - 1], src[n + 1]
            v, va, vb = vo[n], vo[n - 1], vo[n + 1]
            near = pa + pb + plane_sum(p)
            nearv = va * pa + vb * pb + plane_sum(v * p)
            dst[n] = (0.5 * (v * near + nearv)) * rh[n] + b[n]
            return carry

        lax.fori_loop(H - reach, H + R + reach, row, 0)

    def exchange(buf, turn, depth):
        upward = remote(buf.at[H:H + depth], buf.at[H + R:H + R + depth], pr_send.at[2 * turn], pr_recv.at[2 * turn], prev_id)
        downward = remote(
            buf.at[H + R - depth:H + R], buf.at[H - depth:H], pr_send.at[2 * turn + 1], pr_recv.at[2 * turn + 1], next_id
        )

        @pl.when(has_prev)
        def _():
            upward.start()

        @pl.when(has_next)
        def _():
            downward.start()

        @pl.when(has_next)
        def _():
            upward.wait_recv()

        @pl.when(has_prev)
        def _():
            downward.wait_recv()

        return upward, downward

    turn0 = exchange(b, 0, H)
    sweep(b, t0, 3)
    sweep(t0, t1, 2)
    sweep(t1, t0, 1)
    sweep(t0, pm, 0)
    turn1 = exchange(pm, 1, H)
    sweep(pm, t0, 3)
    sweep(t0, t1, 2)
    sweep(t1, pf, 1)

    home = x // C
    block = lax.rem(x, C) * K + k
    spot_rows = pl.ds(block * R, R)
    outs = []
    for e in range(G):
        target = lax.rem(x + e, G)
        src = pf.at[H:H + R, :, pl.ds(pl.multiple_of(target * W, W), W)]
        dst = po.at[spot_rows]
        far = remote(src, dst, out_send.at[e], out_recv.at[block], {"gx": target, "gy": home})
        if e == 0:
            near = pltpu.make_async_copy(src, dst, out_recv.at[block])

            @pl.when(home != k)
            def _(far=far):
                far.start()

            @pl.when(home == k)
            def _(near=near):
                near.start()
        else:
            far.start()
        outs.append(far)

    def slope_row(i, carry):
        n = H + i
        p = pf[n]
        g0 = 0.5 * (pf[n + 1] - pf[n - 1])
        g1 = 0.5 * (right(p) - left(p))
        g2 = 0.5 * (above(p) - below(p))
        for which, g in enumerate((g0, g1, g2)):
            grad_out[which, i] = g
            vel_out[which, i] = pred[which, i + 1] - time_step * g
        return carry

    lax.fori_loop(0, R, slope_row, 0)

    @pl.when(k > 0)
    def _():
        to_up.wait_send()

    @pl.when(k < K - 1)
    def _():
        to_down.wait_send()

    for pair in first:
        for copy in pair:
            copy.wait_send()
    for target, far0, far1 in second:
        @pl.when(target != x)
        def _(far0=far0, far1=far1):
            far0.wait_send()
            far1.wait_send()

    @pl.when(has_prev)
    def _():
        for copy in halo_up + [turn0[0], turn1[0]]:
            copy.wait_send()

    @pl.when(has_next)
    def _():
        for copy in halo_down + [turn0[1], turn1[1]]:
            copy.wait_send()

    for e, far in enumerate(outs):
        if e == 0:
            @pl.when(home != k)
            def _(far=far):
                far.wait_send()
        else:
            far.wait_send()

    for n in range(B):
        here = {"gx": x, "gy": k}
        remote(pf.at[H:H + R, :, 0:W], po.at[n * R:(n + 1) * R], out_send.at[0], out_recv.at[n], here).wait_recv()
    press_out[...] = po[...]


def shards(K, G, particle_count, drag_coeff, particle_velocity, fluid_velocity):
    NZ, R, NY = particle_count.shape
    rows, W = fluid_velocity.shape[2:]
    C = G // K
    H = ROUNDS[0]
    f32 = jnp.float32

    def turned(values):
        return jnp.swapaxes(values, -3, -2)

    dma = pltpu.SemaphoreType.DMA
    pad = (R + 2 * H, NZ, NY)
    scratch = [
        pltpu.VMEM((3, rows + 4, NZ, W), f32),
        pltpu.VMEM((K - 1, C, R + 4, NZ, W), f32),
        pltpu.VMEM((K - 1, C, 2, R + 2, NZ, W), f32),
        pltpu.VMEM((R + 4, NZ, NY), f32),
        pltpu.VMEM((2, R + 2, NZ, NY), f32),
        pltpu.VMEM(pad, jnp.int32),
        pltpu.VMEM((R + 2, NZ, NY), f32),
        pltpu.VMEM((R + 2, NZ, NY), f32),
        pltpu.VMEM((2, R, NZ, NY), f32),
        pltpu.VMEM(pad, f32),
        pltpu.VMEM(pad, f32),
        pltpu.VMEM((3, R + 2, NZ, NY), f32),
        pltpu.VMEM((R + 2, NZ, NY), f32),
        pltpu.VMEM(pad, f32),
        pltpu.VMEM(pad, f32),
        pltpu.VMEM(pad, f32),
        pltpu.VMEM(pad, f32),
        pltpu.VMEM(pad, f32),
        pltpu.VMEM((rows, NZ, W), f32),
        dma((5,)), dma((2,)), dma((2,)),
        dma(((K - 1) * C * 2,)), dma(((K - 1) * C * 2,)),
        dma((K * C * 2,)), dma((G * 2,)),
        dma((6,)), dma((6,)), dma((4,)), dma((4,)), dma((G,)), dma((C * K,)),
    ]
    vmem = pl.BlockSpec(memory_space=pltpu.VMEM)
    anywhere = pl.BlockSpec(memory_space=pl.ANY)
    pressure, velocity, slopes = pl.pallas_call(
        functools.partial(kernel, K, G, R, NZ, NY, W),
        out_shape=(
            jax.ShapeDtypeStruct((rows, NZ, W), f32),
            jax.ShapeDtypeStruct((3, R, NZ, NY), f32),
            jax.ShapeDtypeStruct((3, R, NZ, NY), f32),
        ),
        in_specs=[anywhere] * 4,
        out_specs=(vmem, vmem, vmem),
        scratch_shapes=scratch,
        compiler_params=pltpu.CompilerParams(has_side_effects=True, vmem_limit_bytes=48 * 1024 * 1024),
    )(turned(particle_count), turned(drag_coeff), turned(particle_velocity), turned(fluid_velocity))
    return turned(pressure), turned(velocity), turned(slopes)


def solution(mesh):
    placed = (
        P(None, ("gx", "gy"), None),
        P(None, ("gx", "gy"), None),
        P(None, None, ("gx", "gy"), None),
        P(None, None, "gy", "gx"),
    )
    return jax.shard_map(
        functools.partial(shards, mesh.shape["gy"], mesh.shape["gx"]),
        mesh=mesh,
        in_specs=placed,
        out_specs=(
            P(None, "gy", "gx"),
            P(None, None, ("gx", "gy"), None),
            P(None, None, ("gx", "gy"), None),
        ),
        check_vma=False,
    )
```

time: 202 us -> 96.4 us (0.48)
  Pallas kernels: 0 us -> 88.2 us
  starting transfers between devices: 74.5 us -> 0 us
  waiting for transfers between devices: 67.8 us -> 0 us
  blocking collectives: 26.5 us -> 0 us
  local copies, waits for them, and re-layouts: 21.6 us -> 7.3 us
  other arithmetic: 9.39 us -> 0 us
    pallas_call x0 -> x1, Pallas kernels: none -> 88.2 us  [shards(): pl.pallas_call(functools.partial(kernel, K, G, R, NZ, NY, W), out_shape=(...]
    ppermute x20 -> x0, starting transfers between devices: 46.6 us -> none  [the longest x10 33.7 us: padded_2(): lax.ppermute(tail, axis, [(i, (i + 1) % count) for i in range(ends)])]
    ppermute x20 -> x0, waiting for transfers between devices: 43.7 us -> none  [the longest x10 40.5 us: padded_2(): lax.ppermute(head, axis, [((i + 1) % count, i) for i in range(ends)])]
    all_to_all x3 -> x0, starting transfers between devices: 27.9 us -> none  [the longest x1 18.5 us: to_fluid(): lax.all_to_all(fields, 'gx', split_axis=3, concat_axis=2, tiled=True)]
    all_to_all x1 -> x0, blocking collectives: 26.5 us -> none  [to_particles(): lax.all_to_all(ordered, 'gy', split_axis=2, concat_axis=2, tiled=True)]
    all_to_all x3 -> x0, waiting for transfers between devices: 24.1 us -> none  [the longest x1 12.2 us: to_particles(): lax.all_to_all(lax.all_to_all(ordered, 'gy', split_axis=2, concat_axis=2,...]
    unnamed x10 -> x11, local copies, waits for them, and re-layouts: 12.1 us -> 7.3 us
    all_to_all x4 -> x0, local copies, waits for them, and re-layouts: 4.09 us -> none  [the longest x2 3.96 us: to_fluid(): lax.all_to_all(fields, 'gx', split_axis=3, concat_axis=2, tiled=True)]
  transfers between devices with their start and end apart: 23 -> 0, of which waited for: 20 -> 0; matrix products, arithmetic and copies ran while one was open for 5% -> 0% of each run, Pallas kernels for 0% -> 0%
where the time goes in v1:
time: 96.4 us; the launch traced here: 96.2 us
  Pallas kernels  88.2 us (91%)
  local copies, waits for them, and re-layouts  7.3 us (8%)
    pallas_call x1, Pallas kernels, shards(): pl.pallas_call(functools.partial(kernel, K, G, R, NZ, NY, W), out_shape=(...  88.2 us
    unnamed x11, local copies, waits for them, and re-layouts  7.3 us

profile of v1, /device:TPU:0, one launch (start us, length us, event | category | flops | bytes accessed | tf_op | source)
XLA Modules:
  0.0 96.2 jit_solution(10947415347298304803)
XLA Ops:
  0.6 0.0 copy-start
  0.6 1.2 %copy.21 = s32[8,8,1024]{2,0,1:T(8,128)S(1)} copy(s32[8,8,1024]{2,1,0:T(8,128)} %param.4) | data formatting | bytes 524288 | tf_op args[0]
  1.8 1.1 %copy.20 = f32[8,8,1024]{2,0,1:T(8,128)S(1)} copy(f32[8,8,1024]{2,1,0:T(8,128)} %param.5) | data formatting | bytes 524288 | tf_op args[1]
  2.9 0.0 copy-done
  2.9 0.0 copy-start.1
  3.0 0.5 copy.19
  3.4 0.7 copy-done.1
  4.1 0.5 copy.18
  4.5 88.2 %shard_map.67 = (f32[64,8,128]{2,1,0:T(8,128)S(1)}, f32[3,8,8,1024]{3,2,1,0:T(8,128)S(1)}, f32[3,8,8,1024]{3,2,1,0:T(8,128)S(1)}) custom-call(s32[8,8,1024]{2,1,0:T(8,128)S(1)} %bitcast.17, f32[8,8,1024]{2,1,0:T(8,128)S(1)} %bitcast.18, f32[3,8,8,1024]{3,2,1,0:T(8,128)S(1)} %bitcast.15, f32[3,64,8,128]{3,2,1,0:T(8,128)S(1)} %bitcast.16), custom_call_target="tpu_custom_call" | custom-call | tf_op jit(solution)/shard_map/pallas_call | solution.py:420
  92.7 0.8 copy.11
  93.5 1.3 %copy.12 = f32[3,8,8,1024]{3,2,1,0:T(8,128)} copy(f32[3,8,8,1024]{3,1,2,0:T(8,128)S(1)} %bitcast.20) | data formatting | bytes 1572864
  94.8 1.3 %copy.13 = f32[3,8,8,1024]{3,2,1,0:T(8,128)} copy(f32[3,8,8,1024]{3,1,2,0:T(8,128)S(1)} %bitcast.19) | data formatting | bytes 1572864
Async XLA Ops:
  0.6 2.3 %copy-start = (f32[3,8,8,1024]{3,2,1,0:T(8,128)S(1)}, f32[3,8,8,1024]{3,2,1,0:T(8,128)}, u32[]{:S(2)}) copy-start(f32[3,8,8,1024]{3,2,1,0:T(8,128)} %param.6) | copy-start | bytes 2359300
  2.9 1.1 %copy-start.1 = (f32[3,8,64,128]{3,2,1,0:T(8,128)S(1)}, f32[3,8,64,128]{3,2,1,0:T(8,128)}, u32[]{:S(2)}) copy-start(f32[3,8,64,128]{3,2,1,0:T(8,128)} %param.7) | copy-start | bytes 2359300

commit v2 on v1

v2 whole, which is shorter than its diff:
```python
import functools

import jax
import jax.numpy as jnp
from jax import lax
from jax.experimental import pallas as pl
from jax.experimental.pallas import tpu as pltpu
from jax.sharding import PartitionSpec as P

SWEEPS = 8
ROUNDS = (4, 4)

particle_volume = 0.05
time_step = 0.5
viscosity = 0.1


def kernel(
    K, G, R, NZ, NY, W,
    count_in, drag_in, pvel_in, fluid_in,
    press_out, vel_out, grad_out,
    fp, zb, ub, cn, dr, pv, vo, rh, pred, gr, fl, fr, t0, t1, pf, po,
    loc_sem, fh_send, fh_recv, s1_send, s1_recv, s2_send, s2_recv,
    hal_send, hal_recv, pr_send, pr_recv, out_send, out_recv, *stages,
):
    H = max(ROUNDS)
    b = stages[0]
    C = G // K
    B = C * K
    x = lax.axis_index("gx")
    k = lax.axis_index("gy")
    place = x * K + k
    has_prev = place > 0
    has_next = place < G * K - 1
    prev_id = {"gx": jnp.where(k > 0, x, jnp.maximum(x - 1, 0)), "gy": lax.rem(k + K - 1, K)}
    next_id = {"gx": jnp.where(k < K - 1, x, jnp.minimum(x + 1, G - 1)), "gy": lax.rem(k + 1, K)}

    def remote(src, dst, ssem, rsem, to):
        return pltpu.make_async_remote_copy(
            src_ref=src, dst_ref=dst, send_sem=ssem, recv_sem=rsem, device_id=to, device_id_type=pl.DeviceIdType.MESH
        )

    rows = R * B

    local = [[] for _ in range(4)]
    for z in range(NZ):
        local[0].append(pltpu.make_async_copy(fluid_in.at[:, z], fp.at[:, 1:rows + 1, z], loc_sem.at[z]))
        local[1].append(pltpu.make_async_copy(count_in.at[z], cn.at[H:H + R, z], loc_sem.at[NZ + z]))
        local[2].append(pltpu.make_async_copy(drag_in.at[z], dr.at[:, z], loc_sem.at[2 * NZ + z]))
        local[3].append(pltpu.make_async_copy(pvel_in.at[:, z], pv.at[:, :, z], loc_sem.at[3 * NZ + z]))
    for copies in local:
        for copy in copies:
            copy.start()

    home = x // C
    barrier = pltpu.get_barrier_semaphore()

    def greet(to):
        pl.semaphore_signal(barrier, inc=1, device_id=to, device_id_type=pl.DeviceIdType.MESH)

    for d in range(1, K):
        greet({"gx": x, "gy": lax.rem(k + d, K)})
    for e in range(1, G):
        greet({"gx": lax.rem(x + e, G), "gy": k})

    @pl.when(has_prev)
    def _():
        greet(prev_id)

    @pl.when(has_next)
    def _():
        greet(next_id)

    for c in range(C):
        for j in range(K):
            @pl.when(jnp.logical_or(k * C + c != x, k != j))
            def _(c=c, j=j):
                greet({"gx": k * C + c, "gy": jnp.int32(j)})

    one = jnp.int32(1)
    nothing = jnp.int32(0)
    heard = (
        K + G - 2 + G
        + jnp.where(has_prev, one, nothing)
        + jnp.where(has_next, one, nothing)
        - jnp.where(home == k, one, nothing)
    )

    @pl.when(k == 0)
    def _():
        fp[:, 0:1] = jnp.zeros((3, 1, NZ, W), jnp.float32)

    @pl.when(k == K - 1)
    def _():
        fp[:, rows + 1:rows + 2] = jnp.zeros((3, 1, NZ, W), jnp.float32)

    line = jnp.zeros((NZ, NY), jnp.float32)
    fl[0] = line
    fl[R + 1] = line
    edge = jnp.zeros((H, NZ, NY), jnp.float32)

    @pl.when(jnp.logical_not(has_prev))
    def _():
        fr[0] = line
        for buf in stages:
            buf[0:H] = edge

    @pl.when(jnp.logical_not(has_next))
    def _():
        fr[1] = line
        for buf in stages:
            buf[H + R:2 * H + R] = edge

    for copy in local[0]:
        copy.wait()
    pl.semaphore_wait(barrier, heard)

    up = {"gx": x, "gy": lax.rem(k + K - 1, K)}
    down = {"gx": x, "gy": lax.rem(k + 1, K)}
    to_up = remote(fp.at[:, 1:2], fp.at[:, rows + 1:rows + 2], fh_send.at[0], fh_recv.at[0], up)
    to_down = remote(fp.at[:, rows:rows + 1], fp.at[:, 0:1], fh_send.at[1], fh_recv.at[1], down)

    @pl.when(k > 0)
    def _():
        to_up.start()

    @pl.when(k < K - 1)
    def _():
        to_down.start()

    def part(at):
        return fp.at[:, pl.ds(at * R, R + 2)]

    def at_edge(c, j):
        low = (j == 0) if c == 0 else (j < 0)
        high = (j == K - 1) if c == C - 1 else (j < 0)
        return jnp.logical_or(low, high)

    columns = pl.ds(pl.multiple_of(x * W, W), W)

    def relay(d, c):
        source = lax.rem(k + K - d, K)
        target = source * C + c
        n = d * C + c
        src = part(c * K + k) if d == 0 else zb.at[d - 1, c]
        dst = ub.at[:, :, :, columns]
        far = remote(src, dst, s2_send.at[n], s2_recv.at[x], {"gx": target, "gy": k})
        near = pltpu.make_async_copy(src, dst, s2_recv.at[x])
        return target, far, near

    def pass_on(target, far, near):
        @pl.when(target != x)
        def _():
            far.start()

        @pl.when(target == x)
        def _():
            near.start()

    first = []
    for d in range(1, K):
        j = lax.rem(k + d, K)
        for c in range(C):
            n = (d - 1) * C + c
            first.append((c, j, remote(part(c * K + j), zb.at[d - 1, c], s1_send.at[n], s1_recv.at[n], {"gx": x, "gy": j})))
    second = [[relay(d, c) for c in range(C)] for d in range(K)]

    for c, j, copy in first:
        @pl.when(jnp.logical_not(at_edge(c, j)))
        def _(copy=copy):
            copy.start()

    for c in range(C):
        @pl.when(jnp.logical_not(at_edge(c, k)))
        def _(c=c):
            pass_on(*second[0][c])

    @pl.when(k < K - 1)
    def _():
        to_up.wait_recv()

    @pl.when(k > 0)
    def _():
        to_down.wait_recv()

    for c, j, copy in first:
        @pl.when(at_edge(c, j))
        def _(copy=copy):
            copy.start()

    for c in range(C):
        @pl.when(at_edge(c, k))
        def _(c=c):
            pass_on(*second[0][c])

    halo_up = [remote(cn.at[H:2 * H], cn.at[H + R:2 * H + R], hal_send.at[0], hal_recv.at[0], prev_id)]
    halo_down = [remote(cn.at[R:R + H], cn.at[0:H], hal_send.at[1], hal_recv.at[1], next_id)]

    for copies in local[1:]:
        for copy in copies:
            copy.wait()

    @pl.when(has_prev)
    def _():
        for copy in halo_up:
            copy.start()

    @pl.when(has_next)
    def _():
        for copy in halo_down:
            copy.start()

    for d in range(1, K):
        for c in range(C):
            first[(d - 1) * C + c][2].wait_recv()
            pass_on(*second[d][c])

    @pl.when(has_next)
    def _():
        for copy in halo_up:
            copy.wait_recv()

    @pl.when(has_prev)
    def _():
        for copy in halo_down:
            copy.wait_recv()

    lane = lax.broadcasted_iota(jnp.int32, (NZ, NY), 1)
    level = lax.broadcasted_iota(jnp.int32, (NZ, NY), 0)

    def above(v):
        return jnp.where(level < NZ - 1, pltpu.roll(v, NZ - 1, 0), 0.0)

    def below(v):
        return jnp.where(level > 0, pltpu.roll(v, 1, 0), 0.0)

    def right(v):
        return jnp.where(lane < NY - 1, pltpu.roll(v, NY - 1, 1), 0.0)

    def left(v):
        return jnp.where(lane > 0, pltpu.roll(v, 1, 1), 0.0)

    def plane_sum(v):
        return above(v) + below(v) + right(v) + left(v)

    def inside(i):
        at = place * R + i
        return jnp.logical_and(at >= 0, at < G * K * R)

    def voids_row(n, carry):
        v = 1.0 - cn[n].astype(jnp.float32) * particle_volume
        vo[n] = jnp.where(inside(n - H), v, 0.0)
        return carry

    lax.fori_loop(0, R + 2 * H, voids_row, 0)

    def weight_row(n, carry):
        v = vo[n]
        ws = 0.5 * (6.0 * v + vo[n - 1] + vo[n + 1] + plane_sum(v))
        rh[n] = jnp.where(inside(n - H), 1.0 / ws, 0.0)
        return carry

    lax.fori_loop(1, R + 2 * H - 1, weight_row, 0)

    for sender in range(G):
        spot = pl.ds(sender * W, W)
        here = {"gx": x, "gy": k}
        remote(zb.at[0, 0], ub.at[:, :, :, spot], s2_send.at[0], s2_recv.at[sender], here).wait_recv()

    def momentum_row(i, carry):
        v, va, vb = vo[H + i], vo[H + i - 1], vo[H + i + 1]
        ws = 0.5 * (6.0 * v + va + vb + plane_sum(v))
        drag = dr[i]
        below_line = 1.0 / (v + time_step * drag)
        for which in range(3):
            u, ua, ub_ = ub[which, i + 1], ub[which, i], ub[which, i + 2]
            near = ua + ub_ + plane_sum(u)
            nearv = va * ua + vb * ub_ + plane_sum(v * u)
            diffusion = 0.5 * (v * near + nearv) - ws * u
            force = drag * pv[which, i]
            value = (v * u + (time_step * viscosity) * diffusion + time_step * force) * below_line
            pred[which, i] = value
            f = v * value
            if which == 0:
                fl[i + 1] = f
            elif which == 1:
                part_source = right(f) - left(f)
            else:
                b[H + i] = part_source + (above(f) - below(f))
        return carry

    lax.fori_loop(0, R, momentum_row, 0)

    def source_row(i, carry):
        b[H + i] = -(fl[i + 2] - fl[i] + b[H + i]) * rh[H + i]
        return carry

    lax.fori_loop(0, R, source_row, 0)

    def sweep(src, dst, reach):
        def row(n, carry):
            p, pa, pb = src[n], src[n - 1], src[n + 1]
            v, va, vb = vo[n], vo[n - 1], vo[n + 1]
            near = pa + pb + plane_sum(p)
            nearv = va * pa + vb * pb + plane_sum(v * p)
            dst[n] = (0.5 * (v * near + nearv)) * rh[n] + b[n]
            return carry

        lax.fori_loop(H - reach, H + R + reach, row, 0)

    def exchange(turn, depth):
        buf = stages[turn]
        upward = [
            remote(buf.at[H:H + depth], buf.at[H + R:H + R + depth], pr_send.at[2 * turn], pr_recv.at[2 * turn], prev_id)
        ]
        downward = [
            remote(
                buf.at[H + R - depth:H + R], buf.at[H - depth:H], pr_send.at[2 * turn + 1], pr_recv.at[2 * turn + 1], next_id
            )
        ]
        if turn == 0:
            upward.append(remote(fl.at[1], fr.at[1], hal_send.at[2], hal_recv.at[2], prev_id))
            downward.append(remote(fl.at[R], fr.at[0], hal_send.at[3], hal_recv.at[3], next_id))

        @pl.when(has_prev)
        def _():
            for copy in upward:
                copy.start()

        @pl.when(has_next)
        def _():
            for copy in downward:
                copy.start()

        @pl.when(has_prev)
        def _():
            for copy in upward:
                copy.wait_send()

        @pl.when(has_next)
        def _():
            for copy in downward:
                copy.wait_send()

        @pl.when(has_next)
        def _():
            for copy in upward:
                copy.wait_recv()

        @pl.when(has_prev)
        def _():
            for copy in downward:
                copy.wait_recv()

    done = 0
    for turn, depth in enumerate(ROUNDS):
        exchange(turn, depth)
        if turn == 0:
            b[H] = b[H] + fr[0] * rh[H]
            b[H + R - 1] = b[H + R - 1] - fr[1] * rh[H + R - 1]
            b[H - 1] = b[H - 1] - fl[1] * rh[H - 1]
            b[H + R] = b[H + R] + fl[R] * rh[H + R]
        src = stages[turn]
        for reach in range(depth - 1, -1, -1):
            done += 1
            if done == SWEEPS:
                break
            if done == SWEEPS - 1:
                dst = pf
            elif reach == 0:
                dst = stages[turn + 1]
            else:
                dst = t1 if src is t0 else t0
            sweep(src, dst, reach)
            src = dst

    block = lax.rem(x, C) * K + k
    spot_rows = pl.ds(block * R, R)
    outs = []
    for e in range(G):
        target = lax.rem(x + e, G)
        src = pf.at[H:H + R, :, pl.ds(pl.multiple_of(target * W, W), W)]
        dst = po.at[spot_rows]
        far = remote(src, dst, out_send.at[e], out_recv.at[block], {"gx": target, "gy": home})
        if e == 0:
            near = pltpu.make_async_copy(src, dst, out_recv.at[block])

            @pl.when(home != k)
            def _(far=far):
                far.start()

            @pl.when(home == k)
            def _(near=near):
                near.start()
        else:
            far.start()
        outs.append(far)

    def slope_row(i, carry):
        n = H + i
        p = pf[n]
        g0 = 0.5 * (pf[n + 1] - pf[n - 1])
        g1 = 0.5 * (right(p) - left(p))
        g2 = 0.5 * (above(p) - below(p))
        for which, g in enumerate((g0, g1, g2)):
            gr[which, i] = g
            pred[which, i] = pred[which, i] - time_step * g
        return carry

    lax.fori_loop(0, R, slope_row, 0)
    written = []
    for z in range(NZ):
        written.append(pltpu.make_async_copy(gr.at[:, :, z], grad_out.at[:, z], loc_sem.at[z]))
        written.append(pltpu.make_async_copy(pred.at[:, :, z], vel_out.at[:, z], loc_sem.at[NZ + z]))
    for copy in written:
        copy.start()

    @pl.when(k > 0)
    def _():
        to_up.wait_send()

    @pl.when(k < K - 1)
    def _():
        to_down.wait_send()

    for c, j, copy in first:
        copy.wait_send()
    for pair in second:
        for target, far, near in pair:
            @pl.when(target != x)
            def _(far=far):
                far.wait_send()

    @pl.when(has_prev)
    def _():
        for copy in halo_up:
            copy.wait_send()

    @pl.when(has_next)
    def _():
        for copy in halo_down:
            copy.wait_send()

    for e, far in enumerate(outs):
        if e == 0:
            @pl.when(home != k)
            def _(far=far):
                far.wait_send()
        else:
            far.wait_send()

    for n in range(B):
        here = {"gx": x, "gy": k}
        remote(pf.at[H:H + R, :, 0:W], po.at[n * R:(n + 1) * R], out_send.at[0], out_recv.at[n], here).wait_recv()
    last = [pltpu.make_async_copy(po.at[:, z], press_out.at[z], loc_sem.at[2 * NZ + z]) for z in range(NZ)]
    for copy in last:
        copy.start()
    for copy in written + last:
        copy.wait()


def shards(K, G, particle_count, drag_coeff, particle_velocity, fluid_velocity):
    NZ, R, NY = particle_count.shape
    rows, W = fluid_velocity.shape[2:]
    C = G // K
    H = max(ROUNDS)
    f32 = jnp.float32

    dma = pltpu.SemaphoreType.DMA
    pad = (R + 2 * H, NZ, NY)
    scratch = [
        pltpu.VMEM((3, rows + 2, NZ, W), f32),
        pltpu.VMEM((K - 1, C, 3, R + 2, NZ, W), f32),
        pltpu.VMEM((3, R + 2, NZ, NY), f32),
        pltpu.VMEM(pad, jnp.int32),
        pltpu.VMEM((R, NZ, NY), f32),
        pltpu.VMEM((3, R, NZ, NY), f32),
        pltpu.VMEM(pad, f32),
        pltpu.VMEM(pad, f32),
        pltpu.VMEM((3, R, NZ, NY), f32),
        pltpu.VMEM((3, R, NZ, NY), f32),
        pltpu.VMEM((R + 2, NZ, NY), f32),
        pltpu.VMEM((2, NZ, NY), f32),
        pltpu.VMEM(pad, f32),
        pltpu.VMEM(pad, f32),
        pltpu.VMEM(pad, f32),
        pltpu.VMEM((rows, NZ, W), f32),
        dma((4 * NZ,)), dma((2,)), dma((2,)),
        dma(((K - 1) * C,)), dma(((K - 1) * C,)),
        dma((K * C,)), dma((G,)),
        dma((4,)), dma((4,)), dma((2 * len(ROUNDS),)), dma((2 * len(ROUNDS),)), dma((G,)), dma((C * K,)),
        *[pltpu.VMEM(pad, f32) for _ in ROUNDS],
    ]
    anywhere = pl.BlockSpec(memory_space=pl.ANY)
    return pl.pallas_call(
        functools.partial(kernel, K, G, R, NZ, NY, W),
        out_shape=(
            jax.ShapeDtypeStruct((NZ, rows, W), f32),
            jax.ShapeDtypeStruct((3, NZ, R, NY), f32),
            jax.ShapeDtypeStruct((3, NZ, R, NY), f32),
        ),
        in_specs=[anywhere] * 4,
        out_specs=(anywhere, anywhere, anywhere),
        scratch_shapes=scratch,
        compiler_params=pltpu.CompilerParams(collective_id=0, has_side_effects=True, vmem_limit_bytes=48 * 1024 * 1024),
    )(particle_count, drag_coeff, particle_velocity, fluid_velocity)


def solution(mesh):
    placed = (
        P(None, ("gx", "gy"), None),
        P(None, ("gx", "gy"), None),
        P(None, None, ("gx", "gy"), None),
        P(None, None, "gy", "gx"),
    )
    return jax.shard_map(
        functools.partial(shards, mesh.shape["gy"], mesh.shape["gx"]),
        mesh=mesh,
        in_specs=placed,
        out_specs=(
            P(None, "gy", "gx"),
            P(None, None, ("gx", "gy"), None),
            P(None, None, ("gx", "gy"), None),
        ),
        check_vma=False,
    )
```

time: 96.4 us -> 92.8 us (0.963)
  Pallas kernels: 88.2 us -> 85.3 us
    pallas_call x1, Pallas kernels: 88.2 us -> 85.3 us  [shards(): pl.pallas_call(functools.partial(kernel, K, G, R, NZ, NY, W), out_shape=(...]
where the time goes in v2:
time: 92.8 us; the launch traced here: 92.5 us
  Pallas kernels  85.3 us (92%)
  local copies, waits for them, and re-layouts  6.62 us (7%)
    pallas_call x1, Pallas kernels, shards(): pl.pallas_call(functools.partial(kernel, K, G, R, NZ, NY, W), out_shape=(...  85.3 us
    unnamed x11, local copies, waits for them, and re-layouts  6.62 us

profile of v2, /device:TPU:0, one launch (start us, length us, event | category | flops | bytes accessed | tf_op | source)
XLA Modules:
  0.0 92.5 jit_solution(6858662129467529709)
XLA Ops:
  0.6 0.0 copy-start
  0.6 1.1 %copy-done = f32[3,8,8,1024]{3,2,1,0:T(8,128)S(1)} copy-done((f32[3,8,8,1024]{3,2,1,0:T(8,128)S(1)}, f32[3,8,8,1024]{3,2,1,0:T(8,128)}, u32[]{:S(2)}) %copy-start) | copy-done | bytes 786456
  1.8 0.0 copy-start.1
  1.8 1.1 %copy-done.1 = f32[3,8,64,128]{3,2,1,0:T(8,128)S(1)} copy-done((f32[3,8,64,128]{3,2,1,0:T(8,128)S(1)}, f32[3,8,64,128]{3,2,1,0:T(8,128)}, u32[]{:S(2)}) %copy-start.1) | copy-done | bytes 786456
  2.9 0.0 copy-start.2
  2.9 0.9 %copy-done.2 = s32[8,8,1024]{2,1,0:T(8,128)S(1)} copy-done((s32[8,8,1024]{2,1,0:T(8,128)S(1)}, s32[8,8,1024]{2,1,0:T(8,128)}, u32[]{:S(2)}) %copy-start.2) | copy-done | bytes 262168
  3.8 0.0 copy-start.3
  3.9 0.9 %copy-done.3 = f32[8,8,1024]{2,1,0:T(8,128)S(1)} copy-done((f32[8,8,1024]{2,1,0:T(8,128)S(1)}, f32[8,8,1024]{2,1,0:T(8,128)}, u32[]{:S(2)}) %copy-start.3) | copy-done | bytes 262168
  4.8 85.3 %shard_map.67 = (f32[8,64,128]{2,1,0:T(8,128)S(1)}, f32[3,8,8,1024]{3,2,1,0:T(8,128)S(1)}, f32[3,8,8,1024]{3,2,1,0:T(8,128)S(1)}) custom-call(s32[8,8,1024]{2,1,0:T(8,128)S(1)} %copy-done.2, f32[8,8,1024]{2,1,0:T(8,128)S(1)} %copy-done.3, f32[3,8,8,1024]{3,2,1,0:T(8,128)S(1)} %copy-done, f32[3,8,64,128]{3,2,1,0:T(8,128)S(1)} %copy-done.1), custom_call_target="tpu_custom_call" | custom-call | tf_op jit(solution)/shard_map/pallas_call | solution.py:495
  90.1 0.7 copy.10
  90.8 0.9 copy.11
  91.6 0.9 copy.12
Async XLA Ops:
  0.6 1.1 %copy-start = (f32[3,8,8,1024]{3,2,1,0:T(8,128)S(1)}, f32[3,8,8,1024]{3,2,1,0:T(8,128)}, u32[]{:S(2)}) copy-start(f32[3,8,8,1024]{3,2,1,0:T(8,128)} %pvel_in.1) | copy-start | bytes 2359300
  1.8 1.1 %copy-start.1 = (f32[3,8,64,128]{3,2,1,0:T(8,128)S(1)}, f32[3,8,64,128]{3,2,1,0:T(8,128)}, u32[]{:S(2)}) copy-start(f32[3,8,64,128]{3,2,1,0:T(8,128)} %fluid_in.1) | copy-start | bytes 2359300
  2.9 0.9 %copy-start.2 = (s32[8,8,1024]{2,1,0:T(8,128)S(1)}, s32[8,8,1024]{2,1,0:T(8,128)}, u32[]{:S(2)}) copy-start(s32[8,8,1024]{2,1,0:T(8,128)} %count_in.1) | copy-start | bytes 786436
  3.8 0.9 %copy-start.3 = (f32[8,8,1024]{2,1,0:T(8,128)S(1)}, f32[8,8,1024]{2,1,0:T(8,128)}, u32[]{:S(2)}) copy-start(f32[8,8,1024]{2,1,0:T(8,128)} %drag_in.1) | copy-start | bytes 786436

commit v3 on v2

--- a/solution.py
+++ b/solution.py
@@ -19,8 +19,8 @@
     K, G, R, NZ, NY, W,
     count_in, drag_in, pvel_in, fluid_in,
     press_out, vel_out, grad_out,
-    fp, zb, ub, cn, dr, pv, vo, rh, pred, gr, fl, fr, t0, t1, pf, po,
-    loc_sem, fh_send, fh_recv, s1_send, s1_recv, s2_send, s2_recv,
+    fp, ub, cn, dr, pv, vo, total_w, wf, wr, wa, rh, pred, gr, fl, fr, t0, t1, pf, po,
+    loc_sem, fh_send, fh_recv, s2_send, s2_recv,
     hal_send, hal_recv, pr_send, pr_recv, out_send, out_recv, *stages,
 ):
     H = max(ROUNDS)
@@ -60,9 +60,6 @@
 
     for d in range(1, K):
         greet({"gx": x, "gy": lax.rem(k + d, K)})
-    for e in range(1, G):
-        greet({"gx": lax.rem(x + e, G), "gy": k})
-
     @pl.when(has_prev)
     def _():
         greet(prev_id)
@@ -77,13 +74,18 @@
             def _(c=c, j=j):
                 greet({"gx": k * C + c, "gy": jnp.int32(j)})
 
+    for t in range(G):
+        @pl.when(jnp.logical_or(home != k, x != t))
+        def _(t=t):
+            greet({"gx": jnp.int32(t), "gy": home})
+
     one = jnp.int32(1)
     nothing = jnp.int32(0)
     heard = (
-        K + G - 2 + G
+        K - 1 + G + C * K
         + jnp.where(has_prev, one, nothing)
         + jnp.where(has_next, one, nothing)
-        - jnp.where(home == k, one, nothing)
+        - 2 * jnp.where(home == k, one, nothing)
     )
 
     @pl.when(k == 0)
@@ -138,42 +140,30 @@
 
     columns = pl.ds(pl.multiple_of(x * W, W), W)
 
-    def relay(d, c):
-        source = lax.rem(k + K - d, K)
-        target = source * C + c
-        n = d * C + c
-        src = part(c * K + k) if d == 0 else zb.at[d - 1, c]
-        dst = ub.at[:, :, :, columns]
-        far = remote(src, dst, s2_send.at[n], s2_recv.at[x], {"gx": target, "gy": k})
-        near = pltpu.make_async_copy(src, dst, s2_recv.at[x])
-        return target, far, near
-
-    def pass_on(target, far, near):
-        @pl.when(target != x)
-        def _():
-            far.start()
-
-        @pl.when(target == x)
-        def _():
-            near.start()
-
-    first = []
-    for d in range(1, K):
-        j = lax.rem(k + d, K)
+    sends = []
+    for d in range(K):
         for c in range(C):
-            n = (d - 1) * C + c
-            first.append((c, j, remote(part(c * K + j), zb.at[d - 1, c], s1_send.at[n], s1_recv.at[n], {"gx": x, "gy": j})))
-    second = [[relay(d, c) for c in range(C)] for d in range(K)]
-
-    for c, j, copy in first:
-        @pl.when(jnp.logical_not(at_edge(c, j)))
-        def _(copy=copy):
-            copy.start()
-
-    for c in range(C):
-        @pl.when(jnp.logical_not(at_edge(c, k)))
-        def _(c=c):
-            pass_on(*second[0][c])
+            j = lax.rem(k + d, K)
+            target = k * C + c
+            src = part(c * K + j)
+            dst = ub.at[:, :, :, columns]
+            far = remote(src, dst, s2_send.at[d * C + c], s2_recv.at[x], {"gx": target, "gy": j})
+            near = pltpu.make_async_copy(src, dst, s2_recv.at[x])
+            sends.append((c, j, far, near, jnp.logical_and(target == x, j == k)))
+
+    def send_all(edges):
+        for c, j, far, near, mine in sends:
+            want = at_edge(c, j) if edges else jnp.logical_not(at_edge(c, j))
+
+            @pl.when(jnp.logical_and(want, mine))
+            def _(near=near):
+                near.start()
+
+            @pl.when(jnp.logical_and(want, jnp.logical_not(mine)))
+            def _(far=far):
+                far.start()
+
+    send_all(False)
 
     @pl.when(k < K - 1)
     def _():
@@ -183,15 +173,7 @@
     def _():
         to_down.wait_recv()
 
-    for c, j, copy in first:
-        @pl.when(at_edge(c, j))
-        def _(copy=copy):
-            copy.start()
-
-    for c in range(C):
-        @pl.when(at_edge(c, k))
-        def _(c=c):
-            pass_on(*second[0][c])
+    send_all(True)
 
     halo_up = [remote(cn.at[H:2 * H], cn.at[H + R:2 * H + R], hal_send.at[0], hal_recv.at[0], prev_id)]
     halo_down = [remote(cn.at[R:R + H], cn.at[0:H], hal_send.at[1], hal_recv.at[1], next_id)]
@@ -209,11 +191,6 @@
     def _():
         for copy in halo_down:
             copy.start()
-
-    for d in range(1, K):
-        for c in range(C):
-            first[(d - 1) * C + c][2].wait_recv()
-            pass_on(*second[d][c])
 
     @pl.when(has_next)
     def _():
@@ -257,26 +234,34 @@
     def weight_row(n, carry):
         v = vo[n]
         ws = 0.5 * (6.0 * v + vo[n - 1] + vo[n + 1] + plane_sum(v))
+        total_w[n] = ws
         rh[n] = jnp.where(inside(n - H), 1.0 / ws, 0.0)
+        wf[n] = 0.5 * (v + vo[n + 1])
+        wr[n] = jnp.where(lane < NY - 1, 0.5 * (v + pltpu.roll(v, NY - 1, 1)), 0.0)
+        wa[n] = jnp.where(level < NZ - 1, 0.5 * (v + pltpu.roll(v, NZ - 1, 0)), 0.0)
         return carry
 
+    wf[0] = 0.5 * (vo[0] + vo[1])
     lax.fori_loop(1, R + 2 * H - 1, weight_row, 0)
+
+    def weighted(n, p, pa, pb):
+        r, a = wr[n], wa[n]
+        across = r * pltpu.roll(p, NY - 1, 1) + pltpu.roll(r * p, 1, 1)
+        upright = a * pltpu.roll(p, NZ - 1, 0) + pltpu.roll(a * p, 1, 0)
+        return (wf[n - 1] * pa + wf[n] * pb) + (across + upright)
 
     for sender in range(G):
         spot = pl.ds(sender * W, W)
         here = {"gx": x, "gy": k}
-        remote(zb.at[0, 0], ub.at[:, :, :, spot], s2_send.at[0], s2_recv.at[sender], here).wait_recv()
+        remote(part(0), ub.at[:, :, :, spot], s2_send.at[0], s2_recv.at[sender], here).wait_recv()
 
     def momentum_row(i, carry):
-        v, va, vb = vo[H + i], vo[H + i - 1], vo[H + i + 1]
-        ws = 0.5 * (6.0 * v + va + vb + plane_sum(v))
+        v, ws = vo[H + i], total_w[H + i]
         drag = dr[i]
         below_line = 1.0 / (v + time_step * drag)
         for which in range(3):
-            u, ua, ub_ = ub[which, i + 1], ub[which, i], ub[which, i + 2]
-            near = ua + ub_ + plane_sum(u)
-            nearv = va * ua + vb * ub_ + plane_sum(v * u)
-            diffusion = 0.5 * (v * near + nearv) - ws * u
+            u = ub[which, i + 1]
+            diffusion = weighted(H + i, u, ub[which, i], ub[which, i + 2]) - ws * u
             force = drag * pv[which, i]
             value = (v * u + (time_step * viscosity) * diffusion + time_step * force) * below_line
             pred[which, i] = value
@@ -299,11 +284,7 @@
 
     def sweep(src, dst, reach):
         def row(n, carry):
-            p, pa, pb = src[n], src[n - 1], src[n + 1]
-            v, va, vb = vo[n], vo[n - 1], vo[n + 1]
-            near = pa + pb + plane_sum(p)
-            nearv = va * pa + vb * pb + plane_sum(v * p)
-            dst[n] = (0.5 * (v * near + nearv)) * rh[n] + b[n]
+            dst[n] = weighted(n, src[n], src[n - 1], src[n + 1]) * rh[n] + b[n]
             return carry
 
         lax.fori_loop(H - reach, H + R + reach, row, 0)
@@ -423,13 +404,10 @@
     def _():
         to_down.wait_send()
 
-    for c, j, copy in first:
-        copy.wait_send()
-    for pair in second:
-        for target, far, near in pair:
-            @pl.when(target != x)
-            def _(far=far):
-                far.wait_send()
+    for c, j, far, near, mine in sends:
+        @pl.when(jnp.logical_not(mine))
+        def _(far=far):
+            far.wait_send()
 
     @pl.when(has_prev)
     def _():
@@ -470,13 +448,11 @@
     pad = (R + 2 * H, NZ, NY)
     scratch = [
         pltpu.VMEM((3, rows + 2, NZ, W), f32),
-        pltpu.VMEM((K - 1, C, 3, R + 2, NZ, W), f32),
         pltpu.VMEM((3, R + 2, NZ, NY), f32),
         pltpu.VMEM(pad, jnp.int32),
         pltpu.VMEM((R, NZ, NY), f32),
         pltpu.VMEM((3, R, NZ, NY), f32),
-        pltpu.VMEM(pad, f32),
-        pltpu.VMEM(pad, f32),
+        *[pltpu.VMEM(pad, f32) for _ in range(6)],
         pltpu.VMEM((3, R, NZ, NY), f32),
         pltpu.VMEM((3, R, NZ, NY), f32),
         pltpu.VMEM((R + 2, NZ, NY), f32),
@@ -486,7 +462,6 @@
         pltpu.VMEM(pad, f32),
         pltpu.VMEM((rows, NZ, W), f32),
         dma((4 * NZ,)), dma((2,)), dma((2,)),
-        dma(((K - 1) * C,)), dma(((K - 1) * C,)),
         dma((K * C,)), dma((G,)),
         dma((4,)), dma((4,)), dma((2 * len(ROUNDS),)), dma((2 * len(ROUNDS),)), dma((G,)), dma((C * K,)),
         *[pltpu.VMEM(pad, f32) for _ in ROUNDS],
@@ -502,7 +477,7 @@
         in_specs=[anywhere] * 4,
         out_specs=(anywhere, anywhere, anywhere),
         scratch_shapes=scratch,
-        compiler_params=pltpu.CompilerParams(collective_id=0, has_side_effects=True, vmem_limit_bytes=48 * 1024 * 1024),
+        compiler_params=pltpu.CompilerParams(collective_id=0, has_side_effects=True, vmem_limit_bytes=67043328),
     )(particle_count, drag_coeff, particle_velocity, fluid_velocity)
 
 

time: 92.8 us -> 82.9 us (0.89)
  Pallas kernels: 85.3 us -> 77.3 us
  local copies, waits for them, and re-layouts: 6.62 us -> 4.72 us
    pallas_call x1, Pallas kernels: 85.3 us -> 77.3 us  [shards(): pl.pallas_call(functools.partial(kernel, K, G, R, NZ, NY, W), out_shape=(...]
    unnamed x11 -> x5, local copies, waits for them, and re-layouts: 6.62 us -> 4.72 us
where the time goes in v3:
time: 82.9 us; the launch traced here: 82.7 us
  Pallas kernels  77.3 us (93%)
  local copies, waits for them, and re-layouts  4.72 us (6%)
    pallas_call x1, Pallas kernels, shards(): pl.pallas_call(functools.partial(kernel, K, G, R, NZ, NY, W), out_shape=(...  77.3 us
    unnamed x5, local copies, waits for them, and re-layouts  4.72 us

profile of v3, /device:TPU:0, one launch (start us, length us, event | category | flops | bytes accessed | tf_op | source)
XLA Modules:
  0.0 82.7 jit_solution(12172470120604523470)
XLA Ops:
  0.6 77.3 %shard_map.67 = (f32[8,64,128]{2,1,0:T(8,128)}, f32[3,8,8,1024]{3,2,1,0:T(8,128)}, f32[3,8,8,1024]{3,2,1,0:T(8,128)}) custom-call(s32[8,8,1024]{2,1,0:T(8,128)} %count_in.1, f32[8,8,1024]{2,1,0:T(8,128)} %drag_in.1, f32[3,8,8,1024]{3,2,1,0:T(8,128)} %pvel_in.1, f32[3,8,64,128]{3,2,1,0:T(8,128)} %fluid_in.1), custom_call_target="tpu_custom_call" | custom-call | tf_op jit(solution)/shard_map/pallas_call | solution.py:470
  78.0 1.7 %copy.10 = f32[8,64,128]{2,1,0:T(8,128)} copy(f32[8,64,128]{2,1,0:T(8,128)} %get-tuple-element.6) | data formatting | bytes 524288
  79.6 0.0 copy-start
  79.6 2.2 %copy.11 = f32[3,8,8,1024]{3,2,1,0:T(8,128)} copy(f32[3,8,8,1024]{3,2,1,0:T(8,128)} %get-tuple-element.7) | data formatting | bytes 1572864
  81.8 0.0 copy-done
  81.8 0.9 %copy.12 = f32[3,8,8,1024]{3,2,1,0:T(8,128)} copy(f32[3,8,8,1024]{3,2,1,0:T(8,128)S(1)} %copy-done) | data formatting | bytes 1572864
Async XLA Ops:
  79.6 2.2 %copy-start = (f32[3,8,8,1024]{3,2,1,0:T(8,128)S(1)}, f32[3,8,8,1024]{3,2,1,0:T(8,128)}, u32[]{:S(2)}) copy-start(f32[3,8,8,1024]{3,2,1,0:T(8,128)} %get-tuple-element.8) | copy-start | bytes 2359300
